TPU v7x, 256 devices: a whole 4x4x8 slice. The times are simulated.
256 devices in a mesh: gx: 4 (over x_lo, core), gy: 16 (over x_hi, z), gz: 4 (over y).
Axes of the slice: x: 4 (x_hi: 2, x_lo: 2; x = x_hi * 2 + x_lo), y: 4, z: 8, core: 2. Of those that a mesh axis runs over, the one named last changes fastest.
Arguments:
- field: bfloat16 [64, 8, 384, 1536], P(None, 'gz', 'gy', 'gx'), may hold values from -200 to 200, as said below
- mode_one_factor: bfloat16 [1536, 256], P('gx'), may hold values from -0.15625 to 0.15625
- mode_two_factor: bfloat16 [384, 256], P('gy'), may hold values from -0.3125 to 0.3125
Outputs:
- gram_one: float32 [1536, 1536], P('gx')
- gram_two: float32 [384, 384], P('gy')
- core: bfloat16 [64, 8, 256, 256], P('gx', 'gz', 'gy')
Inputs may be any that keep to these rules, and one draw needn't show every extreme that they name: `field`: the snapshot's values lie within -200 and 200.
All inputs are finite; a program needn't handle non-finite values.
Results may differ from a plain program's by a relative error of at most 0.005.
Values may be sent and summed in bfloat16 or wider, within the bound.
A program may use at most 128 MiB of HBM per device.

v0:
```python
import jax
import jax.numpy as jnp
from jax import lax
from jax.sharding import PartitionSpec as P


def local(field, mode_one_factor, mode_two_factor):
    vars_all, cells_three, cells_two, cells_one = field.shape
    count_gx = lax.axis_size("gx")
    count_gy = lax.axis_size("gy")
    own_rows = vars_all // count_gx
    total_three = cells_three * lax.axis_size("gz")
    total_two = cells_two * count_gy
    rank_one = mode_one_factor.shape[1]
    rank_two = mode_two_factor.shape[1]
    own_ranks = rank_two // count_gy
    factor_one = lax.all_gather(mode_one_factor, "gx", axis=0, tiled=True)
    piece = lax.all_gather(field, "gx", axis=3, tiled=True)
    width = piece.shape[3]
    gram_block = lax.dot_general(
        field.reshape(-1, cells_one),
        piece.reshape(-1, width),
        (((0,), (0,)), ((), ())),
        preferred_element_type=jnp.float32,
    )
    gram_sum = lax.psum(lax.psum(gram_block, "gz"), "gy")
    gram_one = gram_sum * (1.0 / (vars_all * total_three * total_two))
    own_vars = lax.dynamic_slice_in_dim(piece, lax.axis_index("gx") * own_rows, own_rows, axis=0)
    shrunk = (
        jnp.dot(own_vars.reshape(-1, width), factor_one, preferred_element_type=jnp.float32)
        .astype(jnp.bfloat16)
        .reshape(own_rows, cells_three, cells_two, rank_one)
    )
    shrunk_all = lax.all_gather(shrunk, "gy", axis=2, tiled=True)
    gram_two_block = jnp.einsum(
        "akjr,akqr->jq", shrunk, shrunk_all, preferred_element_type=jnp.float32
    )
    gram_two = lax.psum(gram_two_block, ("gx", "gz")) * (1.0 / (vars_all * total_three * rank_one))
    factor_two = lax.all_gather(mode_two_factor, "gy", axis=0, tiled=True)
    own_cols = lax.dynamic_slice_in_dim(
        factor_two, lax.axis_index("gy") * own_ranks, own_ranks, axis=1
    )
    core = jnp.einsum(
        "akjr,js->aksr", shrunk_all, own_cols, preferred_element_type=jnp.float32
    ).astype(jnp.bfloat16)
    return (gram_one, gram_two, core)


def solution(mesh):
    placed = (P(None, "gz", "gy", "gx"), P("gx", None), P("gy", None))
    return jax.shard_map(
        local,
        mesh=mesh,
        in_specs=placed,
        out_specs=(P("gx", None), P("gy", None), P("gx", "gz", "gy", None)),
        check_vma=False,
    )
```

profile of v0, /device:TPU:32, one launch (start us, length us, event | category | flops | bytes accessed | tf_op | source)
XLA Modules:
  0.0 535.0 jit_solution(3255514334234658207)
XLA Ops:
  7.2 0.0 copy-start
  7.2 0.0 all-gather.3.cloned.1.call-start
  7.2 0.7 all-gather.3.cloned.1.call-update
  7.9 0.0 all-reduce.3.cloned.1.call-start
  8.0 95.6 %all-gather.3.cloned.1.call-done = bf16[64,2,24,1536]{3,2,1,0:T(8,128)(2,1)} async-done(((bf16[64,2,24,384]{3,2,1,0:T(8,128)(2,1)}), bf16[64,2,24,1536]{3,2,1,0:T(8,128)(2,1)}) %all-gather.3.cloned.1.call-update) | async-done | bytes 9437200 | tf_op jit(solution)/shard_map/all_gather | solution.py:18
  103.5 0.0 copy-done
  103.5 7.8 %convolution_bitcast_fusion = f32[384,1536]{1,0:T(8,128)} fusion(bf16[64,2,24,384]{3,2,1,0:T(8,128)(2,1)S(1)} %copy-done, bf16[64,2,24,1536]{3,2,1,0:T(8,128)(2,1)} %all-gather.3.cloned.1.call-done), kind=kOutput, calls=%fused_computation | convolution fusion | flops 3623878656 | bytes 14155776 | tf_op jit(solution)/shard_map/dot_general | solution.py:20
  111.4 0.0 copy-start.2
  111.4 0.0 all-reduce.3.cloned.1.call-update
  111.4 0.0 all-reduce.5.cloned.1.call-start
  111.4 70.6 %all-reduce.3.cloned.1.call-done = f32[384,1536]{1,0:T(8,128)} async-done(((f32[384,1536]{1,0:T(8,128)}), f32[384,1536]{1,0:T(8,128)}) %all-reduce.3.cloned.1.call-update) | async-done | bytes 2359312 | tf_op jit(solution)/shard_map/psum | solution.py:26
  182.1 0.0 all-reduce.5.cloned.1.call-update
  182.1 0.0 all-gather.5.cloned.1.call-start
  182.1 0.0 copy-done.2
  182.1 8.6 %all_gather.13 = bf16[1536,256]{1,0:T(8,128)(2,1)S(1)} all-gather(bf16[384,256]{1,0:T(8,128)(2,1)S(1)} %copy-done.2), channel_id=1, replica_groups=mesh['gx'=4,'gy'=16,'gz'=4] {'gx'}, dimensions={0}, use_global_device_ids=true | all-gather | bytes 983040 | tf_op jit(solution)/shard_map/all_gather | solution.py:17
  190.7 1.8 constant_dynamic-slice_fusion
  192.5 0.0 copy-start.3
  192.6 1.5 convolution_convert_fusion
  194.1 0.0 all-gather.5.cloned.1.call-update
  194.1 0.0 copy-done.3
  194.1 38.6 %all_gather.15 = bf16[384,256]{1,0:T(8,128)(2,1)S(1)} all-gather(bf16[24,256]{1,0:T(8,128)(2,1)S(1)} %copy-done.3), channel_id=1, replica_groups=mesh['gx'=4,'gy'=16,'gz'=4] {'gy'}, dimensions={0}, use_global_device_ids=true | all-gather | bytes 208896 | tf_op jit(solution)/shard_map/all_gather | solution.py:39
  232.8 0.0 copy-start.1
  232.8 115.1 %all-reduce.5.cloned.1.call-done = f32[384,1536]{1,0:T(8,128)} async-done(((f32[384,1536]{1,0:T(8,128)}), f32[384,1536]{1,0:T(8,128)}) %all-reduce.5.cloned.1.call-update) | async-done | bytes 2359312 | tf_op jit(solution)/shard_map/psum | solution.py:26
  347.9 3.3 broadcast_multiply_fusion
  351.2 113.4 %all-gather.5.cloned.1.call-done = bf16[16,2,384,256]{3,2,1,0:T(8,128)(2,1)} async-done(((bf16[16,2,24,256]{3,2,1,0:T(8,128)(2,1)}), bf16[16,2,384,256]{3,2,1,0:T(8,128)(2,1)}) %all-gather.5.cloned.1.call-update) | async-done | bytes 6291472 | tf_op jit(solution)/shard_map/all_gather | solution.py:34
  464.6 0.0 copy-done.1
  464.6 4.5 convolution_bitcast_fusion.1
  469.1 54.3 %psum.23 = f32[24,384]{1,0:T(8,128)S(1)} all-reduce(f32[24,384]{1,0:T(8,128)S(1)} %convolution_bitcast_fusion.1), channel_id=1, replica_groups=mesh['gx'=4,'gy'=16,'gz'=4] {'gx','gz'}, use_global_device_ids=true, to_apply=%region_2.0 | all-reduce | flops 9216 | bytes 73728 | tf_op jit(solution)/shard_map/psum | solution.py:38
  523.4 0.6 broadcast_multiply_fusion.1
  524.0 4.5 fusion
Async XLA Ops:
  7.2 96.4 %copy-start = (bf16[64,2,24,384]{3,2,1,0:T(8,128)(2,1)S(1)}, bf16[64,2,24,384]{3,2,1,0:T(8,128)(2,1)}, u32[]{:S(2)}) copy-start(bf16[64,2,24,384]{3,2,1,0:T(8,128)(2,1)} %param.3) | copy-start | bytes 7077892
  7.2 96.4 %all-gather.3.cloned.1.call-start = ((), (), s32[]{:S(2)}) async-start(), calls=%async_computation | async-start | bytes 11796480 | tf_op jit(solution)/shard_map/all_gather | solution.py:18
  7.9 174.2 %all-reduce.3.cloned.1.call-start = ((), (), s32[]{:S(2)}) async-start(), calls=%async_computation.1 | async-start | bytes 4718592 | tf_op jit(solution)/shard_map/psum | solution.py:26
  111.4 70.8 %copy-start.2 = (bf16[384,256]{1,0:T(8,128)(2,1)S(1)}, bf16[384,256]{1,0:T(8,128)(2,1)}, u32[]{:S(2)}) copy-start(bf16[384,256]{1,0:T(8,128)(2,1)} %param.4) | copy-start | bytes 589828
  111.4 236.5 %all-reduce.5.cloned.1.call-start = ((), (), s32[]{:S(2)}) async-start(), calls=%async_computation.2 | async-start | bytes 4718592 | tf_op jit(solution)/shard_map/psum | solution.py:26
  182.1 282.5 %all-gather.5.cloned.1.call-start = ((), (), s32[]{:S(2)}) async-start(), calls=%async_computation.3 | async-start | bytes 6684672 | tf_op jit(solution)/shard_map/all_gather | solution.py:34
  192.5 1.6 copy-start.3
  232.8 231.8 %copy-start.1 = (bf16[768,256]{1,0:T(8,128)(2,1)S(1)}, bf16[768,256]{1,0:T(8,128)(2,1)}, u32[]{:S(2)}) copy-start(bf16[768,256]{1,0:T(8,128)(2,1)} %convolution_convert_fusion) | copy-start | bytes 1179652
Sparse Core Ops, SparseCore 0:
  9.8 93.6 all-gather.2
  111.5 70.5 all-reduce.2
  184.7 163.1 all-reduce.4
  350.4 114.1 all-gather.4
where the time goes:
time: 535 us
  waiting for transfers between devices  396 us (74%)
  blocking collectives  101 us (19%)
  matrix products  18.3 us (3%)
  between operations  13.8 us (3%)
    psum x2, waiting for transfers between devices, local(): gram_sum = lax.psum(lax.psum(gram_block, 'gz'), 'gy')  186 us
    all_gather x1, waiting for transfers between devices, local(): shrunk_all = lax.all_gather(shrunk, 'gy', axis=2, tiled=True)  113 us
    all_gather x1, waiting for transfers between devices, local(): piece = lax.all_gather(field, 'gx', axis=3, tiled=True)  95.6 us
    psum x1, blocking collectives, local(): lax.psum(gram_two_block, ('gx', 'gz'))  54.3 us
    all_gather x1, blocking collectives, local(): factor_two = lax.all_gather(mode_two_factor, 'gy', axis=0, tiled=True)  38.6 us
  transfers between devices with their start and end apart: 4, of which 4 were waited for; matrix products, arithmetic and copies ran while one was open for 1% of the time, Pallas kernels for 0%

commit v1 on v0

--- a/solution.py
+++ b/solution.py
@@ -31,7 +31,8 @@
         .astype(jnp.bfloat16)
         .reshape(own_rows, cells_three, cells_two, rank_one)
     )
-    shrunk_all = lax.all_gather(shrunk, "gy", axis=2, tiled=True)
+    repeated = jnp.stack([shrunk] * lax.axis_size("gy"))
+    shrunk_all = jnp.concatenate(lax.all_to_all(repeated, "gy", 0, 0), axis=2)
     gram_two_block = jnp.einsum(
         "akjr,akqr->jq", shrunk, shrunk_all, preferred_element_type=jnp.float32
     )

time: 535 us -> 460 us (0.86)
  waiting for transfers between devices: 396 us -> 236 us
  blocking collectives: 101 us -> 169 us
  starting transfers between devices: 0.16 us -> 10 us
  local copies, waits for them, and re-layouts: 1.83 us -> 11.5 us
    all_gather x1 -> x0, waiting for transfers between devices: 113 us -> none  [local(): shrunk_all = lax.all_gather(shrunk, 'gy', axis=2, tiled=True)]
    all_gather x1, blocking collectives: 38.6 us -> 107 us  [local(): factor_two = lax.all_gather(mode_two_factor, 'gy', axis=0, tiled=True)]
    psum x2, waiting for transfers between devices: 186 us -> 148 us  [local(): gram_sum = lax.psum(lax.psum(gram_block, 'gz'), 'gy')]
    all_to_all x0 -> x1, starting transfers between devices: none -> 9.89 us  [local(): shrunk_all = jnp.concatenate(lax.all_to_all(repeated, 'gy', 0, 0), axis=2)]
    all_gather x1, waiting for transfers between devices: 95.6 us -> 86.9 us  [local(): piece = lax.all_gather(field, 'gx', axis=3, tiled=True)]
  transfers between devices with their start and end apart: 4 -> 4, of which waited for: 4 -> 3; matrix products, arithmetic and copies ran while one was open for 1% -> 2% of each run, Pallas kernels for 0% -> 0%
where the time goes in v1:
time: 460 us; the launch traced here: 459 us
  waiting for transfers between devices  236 us (51%)
  blocking collectives  169 us (37%)
  matrix products  14.8 us (3%)
  between operations  13.8 us (3%)
  local copies, waits for them, and re-layouts  11.5 us (2%)
  starting transfers between devices  10 us (2%)
    psum x2, waiting for transfers between devices, local(): gram_sum = lax.psum(lax.psum(gram_block, 'gz'), 'gy')  148 us
    all_gather x1, blocking collectives, local(): factor_two = lax.all_gather(mode_two_factor, 'gy', axis=0, tiled=True)  107 us
    all_gather x1, waiting for transfers between devices, local(): piece = lax.all_gather(field, 'gx', axis=3, tiled=True)  86.9 us
    psum x1, blocking collectives, local(): lax.psum(gram_two_block, ('gx', 'gz'))  54.3 us
    all_to_all x1, starting transfers between devices, local(): shrunk_all = jnp.concatenate(lax.all_to_all(repeated, 'gy', 0, 0), axis=2)  9.89 us
  transfers between devices with their start and end apart: 4, of which 3 were waited for; matrix products, arithmetic and copies ran while one was open for 2% of the time, Pallas kernels for 0%

profile of v1, /device:TPU:32, one launch (start us, length us, event | category | flops | bytes accessed | tf_op | source)
XLA Modules:
  0.0 459.3 jit_solution(10355961033012015710)
XLA Ops:
  7.2 0.0 copy-start.2
  7.2 0.0 all-gather.2.cloned.1.call-start
  7.2 0.7 all-gather.2.cloned.1.call-update
  7.9 0.2 copy-done.2
  8.1 8.6 %all_gather.10 = bf16[1536,256]{1,0:T(8,128)(2,1)S(1)} all-gather(bf16[384,256]{1,0:T(8,128)(2,1)S(1)} %copy-done.2), channel_id=1, replica_groups=mesh['gx'=4,'gy'=16,'gz'=4] {'gx'}, dimensions={0}, use_global_device_ids=true | all-gather | bytes 983040 | tf_op jit(solution)/shard_map/all_gather | solution.py:17
  16.7 86.9 %all-gather.2.cloned.1.call-done = bf16[64,2,24,1536]{3,2,1,0:T(8,128)(2,1)} async-done(((bf16[64,2,24,384]{3,2,1,0:T(8,128)(2,1)}), bf16[64,2,24,1536]{3,2,1,0:T(8,128)(2,1)}) %all-gather.2.cloned.1.call-update) | async-done | bytes 9437200 | tf_op jit(solution)/shard_map/all_gather | solution.py:18
  103.5 1.8 constant_dynamic-slice_fusion
  105.4 0.8 convolution_convert_fusion
  106.1 3.2 stack.3
  109.4 0.0 copy-start.1
  109.4 9.9 %all-to-all-start = ((bf16[16,16,2,24,256]{4,3,2,1,0:T(8,128)(2,1)}), bf16[16,16,2,24,256]{4,3,2,1,0:T(8,128)(2,1)}, u32[]{:S(2)}, u32[]{:S(2)}) async-start(bf16[16,16,2,24,256]{4,3,2,1,0:T(8,128)(2,1)} %stack.3), calls=%async_computation | async-start | bytes 12582912 | tf_op jit(solution)/shard_map/all_to_all | solution.py:35
  119.3 0.0 all-reduce.3.cloned.1.call-start
  119.3 0.0 copy-done.1
  119.3 7.8 %convolution_bitcast_fusion = f32[384,1536]{1,0:T(8,128)} fusion(bf16[64,2,24,384]{3,2,1,0:T(8,128)(2,1)S(1)} %copy-done.1, bf16[64,2,24,1536]{3,2,1,0:T(8,128)(2,1)} %all-gather.2.cloned.1.call-done), kind=kOutput, calls=%fused_computation | convolution fusion | flops 3623878656 | bytes 14155776 | tf_op jit(solution)/shard_map/dot_general | solution.py:20
  127.1 0.0 copy-start.3
  127.1 0.0 all-reduce.3.cloned.1.call-update
  127.2 0.0 all-reduce.5.cloned.1.call-start
  127.2 69.9 %all-reduce.3.cloned.1.call-done = f32[384,1536]{1,0:T(8,128)} async-done(((f32[384,1536]{1,0:T(8,128)}), f32[384,1536]{1,0:T(8,128)}) %all-reduce.3.cloned.1.call-update) | async-done | bytes 2359312 | tf_op jit(solution)/shard_map/psum | solution.py:26
  197.2 0.0 all-reduce.5.cloned.1.call-update
  197.2 0.0 copy-done.3
  197.2 106.6 %all_gather.11 = bf16[384,256]{1,0:T(8,128)(2,1)S(1)} all-gather(bf16[24,256]{1,0:T(8,128)(2,1)S(1)} %copy-done.3), channel_id=1, replica_groups=mesh['gx'=4,'gy'=16,'gz'=4] {'gy'}, dimensions={0}, use_global_device_ids=true | all-gather | bytes 208896 | tf_op jit(solution)/shard_map/all_gather | solution.py:40
  303.8 78.3 %all-reduce.5.cloned.1.call-done = f32[384,1536]{1,0:T(8,128)} async-done(((f32[384,1536]{1,0:T(8,128)}), f32[384,1536]{1,0:T(8,128)}) %all-reduce.5.cloned.1.call-update) | async-done | bytes 2359312 | tf_op jit(solution)/shard_map/psum | solution.py:26
  382.1 3.3 broadcast_multiply_fusion
  385.4 0.0 all-to-all-done
  385.4 3.6 copy.13
  389.0 0.0 copy-start
  389.0 2.7 copy-done
  391.6 1.7 convolution_bitcast_fusion.1
  393.4 54.3 %psum.23 = f32[24,384]{1,0:T(8,128)S(1)} all-reduce(f32[24,384]{1,0:T(8,128)S(1)} %convolution_bitcast_fusion.1), channel_id=1, replica_groups=mesh['gx'=4,'gy'=16,'gz'=4] {'gx','gz'}, use_global_device_ids=true, to_apply=%region_2.0 | all-reduce | flops 9216 | bytes 73728 | tf_op jit(solution)/shard_map/psum | solution.py:39
  447.6 0.6 broadcast_multiply_fusion.1
  448.3 4.5 fusion
Async XLA Ops:
  7.2 0.9 copy-start.2
  7.2 96.4 %all-gather.2.cloned.1.call-start = ((), (), s32[]{:S(2)}) async-start(), calls=%async_computation.1 | async-start | bytes 11796480 | tf_op jit(solution)/shard_map/all_gather | solution.py:18
  109.4 9.9 %copy-start.1 = (bf16[64,2,24,384]{3,2,1,0:T(8,128)(2,1)S(1)}, bf16[64,2,24,384]{3,2,1,0:T(8,128)(2,1)}, u32[]{:S(2)}) copy-start(bf16[64,2,24,384]{3,2,1,0:T(8,128)(2,1)} %param.3) | copy-start | bytes 7077892
  109.4 276.0 %all-to-all-start = ((bf16[16,16,2,24,256]{4,3,2,1,0:T(8,128)(2,1)}), bf16[16,16,2,24,256]{4,3,2,1,0:T(8,128)(2,1)}, u32[]{:S(2)}, u32[]{:S(2)}) async-start(bf16[16,16,2,24,256]{4,3,2,1,0:T(8,128)(2,1)} %stack.3), calls=%async_computation | async-start | bytes 12582912 | tf_op jit(solution)/shard_map/all_to_all | solution.py:35
  119.3 77.9 %all-reduce.3.cloned.1.call-start = ((), (), s32[]{:S(2)}) async-start(), calls=%async_computation.2 | async-start | bytes 4718592 | tf_op jit(solution)/shard_map/psum | solution.py:26
  127.1 70.1 %copy-start.3 = (bf16[24,256]{1,0:T(8,128)(2,1)S(1)}, bf16[24,256]{1,0:T(8,128)(2,1)}, u32[]{:S(2)}) copy-start(bf16[24,256]{1,0:T(8,128)(2,1)} %param.5) | copy-start | bytes 36868
  127.2 254.9 %all-reduce.5.cloned.1.call-start = ((), (), s32[]{:S(2)}) async-start(), calls=%async_computation.3 | async-start | bytes 4718592 | tf_op jit(solution)/shard_map/psum | solution.py:26
  389.0 2.7 copy-start
Sparse Core Ops, SparseCore 0:
  9.8 93.6 all-gather.1
  127.3 69.8 all-reduce.2
  199.8 182.2 all-reduce.4

commit v2 on v0

--- a/solution.py
+++ b/solution.py
@@ -1,7 +1,15 @@
+import functools
 import jax
 import jax.numpy as jnp
 from jax import lax
 from jax.sharding import PartitionSpec as P
+
+
+def _show_spots(mat, peer_axis):
+    return jnp.sum(jax.lax.all_gather(mat, peer_axis), axis=0)
+
+
+recover_the_quarters = functools.partial(_show_spots, peer_axis="gz")
 
 
 def local(field, mode_one_factor, mode_two_factor):
@@ -23,7 +31,7 @@
         (((0,), (0,)), ((), ())),
         preferred_element_type=jnp.float32,
     )
-    gram_sum = lax.psum(lax.psum(gram_block, "gz"), "gy")
+    gram_sum = lax.psum(recover_the_quarters(gram_block), "gy")
     gram_one = gram_sum * (1.0 / (vars_all * total_three * total_two))
     own_vars = lax.dynamic_slice_in_dim(piece, lax.axis_index("gx") * own_rows, own_rows, axis=0)
     shrunk = (

time: 535 us -> 503 us (0.940)
  waiting for transfers between devices: 396 us -> 353 us
  other arithmetic: 3.91 us -> 10.3 us
    psum x2 -> x1, waiting for transfers between devices: 186 us -> 99.6 us  [local(): gram_sum = lax.psum(recover_the_quarters(gram_block), 'gy')]
    all_gather x0 -> x1, waiting for transfers between devices: none -> 83.5 us  [_show_spots(): return jnp.sum(jax.lax.all_gather(mat, peer_axis), axis=0)]
    all_gather x1, waiting for transfers between devices: 113 us -> 74 us  [local(): shrunk_all = lax.all_gather(shrunk, 'gy', axis=2, tiled=True)]
    reduce_sum x0 -> x1, other arithmetic: none -> 6.37 us  [_show_spots(): return jnp.sum(jax.lax.all_gather(mat, peer_axis), axis=0)]
  transfers between devices with their start and end apart: 4 -> 4, of which waited for: 4 -> 4; matrix products, arithmetic and copies ran while one was open for 1% -> 4% of each run, Pallas kernels for 0% -> 0%
where the time goes in v2:
time: 503 us; the launch traced here: 502 us
  waiting for transfers between devices  353 us (70%)
  blocking collectives  102 us (20%)
  matrix products  18.4 us (4%)
  between operations  13.8 us (3%)
  other arithmetic  10.3 us (2%)
    psum x1, waiting for transfers between devices, local(): gram_sum = lax.psum(recover_the_quarters(gram_block), 'gy')  99.6 us
    all_gather x1, waiting for transfers between devices, local(): piece = lax.all_gather(field, 'gx', axis=3, tiled=True)  95.6 us
    all_gather x1, waiting for transfers between devices, _show_spots(): return jnp.sum(jax.lax.all_gather(mat, peer_axis), axis=0)  83.5 us
    all_gather x1, waiting for transfers between devices, local(): shrunk_all = lax.all_gather(shrunk, 'gy', axis=2, tiled=True)  74 us
    psum x1, blocking collectives, local(): lax.psum(gram_two_block, ('gx', 'gz'))  54.3 us
    all_gather x1, blocking collectives, local(): factor_two = lax.all_gather(mode_two_factor, 'gy', axis=0, tiled=True)  38.8 us
  transfers between devices with their start and end apart: 4, of which 4 were waited for; matrix products, arithmetic and copies ran while one was open for 4% of the time, Pallas kernels for 0%

profile of v2, /device:TPU:32, one launch (start us, length us, event | category | flops | bytes accessed | tf_op | source)
XLA Modules:
  0.0 501.7 jit_solution(6749816770810435192)
XLA Ops:
  7.2 0.0 copy-start
  7.2 0.0 all-gather.5.cloned.1.call-start
  7.2 0.7 all-gather.5.cloned.1.call-update
  7.9 0.0 all-gather.9.cloned.1.call-start
  8.0 95.6 %all-gather.5.cloned.1.call-done = bf16[64,2,24,1536]{3,2,1,0:T(8,128)(2,1)} async-done(((bf16[64,2,24,384]{3,2,1,0:T(8,128)(2,1)}), bf16[64,2,24,1536]{3,2,1,0:T(8,128)(2,1)}) %all-gather.5.cloned.1.call-update) | async-done | bytes 9437200 | tf_op jit(solution)/shard_map/all_gather | solution.py:26
  103.5 0.0 copy-done
  103.5 7.8 %convolution_bitcast_fusion = f32[384,1536]{1,0:T(8,128)} fusion(bf16[64,2,24,384]{3,2,1,0:T(8,128)(2,1)S(1)} %copy-done, bf16[64,2,24,1536]{3,2,1,0:T(8,128)(2,1)} %all-gather.5.cloned.1.call-done), kind=kOutput, calls=%fused_computation | convolution fusion | flops 3623878656 | bytes 14155776 | tf_op jit(solution)/shard_map/dot_general | solution.py:28
  111.4 0.0 copy-start.2
  111.4 0.0 all-gather.9.cloned.1.call-update
  111.4 0.0 all-gather.7.cloned.1.call-start
  111.4 0.8 copy-done.2
  112.3 9.3 %all_gather.21 = bf16[1536,256]{1,0:T(8,128)(2,1)S(1)} all-gather(bf16[384,256]{1,0:T(8,128)(2,1)S(1)} %copy-done.2), channel_id=1, replica_groups=mesh['gx'=4,'gy'=16,'gz'=4] {'gx'}, dimensions={0}, use_global_device_ids=true | all-gather | bytes 983040 | tf_op jit(solution)/shard_map/all_gather | solution.py:25
  121.6 1.8 constant_dynamic-slice_fusion
  123.4 1.5 convolution_convert_fusion
  124.9 0.0 all-gather.7.cloned.1.call-update
  124.9 0.0 all-reduce.2.cloned.1.call-start
  125.0 83.5 %all-gather.9.cloned.1.call-done = f32[1536,1536]{1,0:T(8,128)} async-done(((f32[384,1536]{1,0:T(8,128)}), f32[1536,1536]{1,0:T(8,128)}) %all-gather.9.cloned.1.call-update) | async-done | bytes 9437200 | tf_op jit(solution)/shard_map/all_gather | solution.py:9
  208.5 6.4 %reduce_sum.9 = f32[384,1536]{1,0:T(8,128)} reduce(f32[4,384,1536]{2,1,0:T(8,128)} %bitcast.26, f32[]{:T(128)} %constant.4.clone.1), dimensions={0}, to_apply=%region_0.0 | reduce | flops 1769472 | bytes 11796484 | tf_op jit(solution)/shard_map/reduce_sum | solution.py:9
  214.8 0.0 copy-start.3
  214.8 0.0 copy-start.1
  214.8 0.0 all-reduce.2.cloned.1.call-update
  214.9 0.7 copy-done.3
  215.5 38.8 %all_gather.23 = bf16[384,256]{1,0:T(8,128)(2,1)S(1)} all-gather(bf16[24,256]{1,0:T(8,128)(2,1)S(1)} %copy-done.3), channel_id=1, replica_groups=mesh['gx'=4,'gy'=16,'gz'=4] {'gy'}, dimensions={0}, use_global_device_ids=true | all-gather | bytes 208896 | tf_op jit(solution)/shard_map/all_gather | solution.py:47
  254.4 74.0 %all-gather.7.cloned.1.call-done = bf16[16,2,384,256]{3,2,1,0:T(8,128)(2,1)} async-done(((bf16[16,2,24,256]{3,2,1,0:T(8,128)(2,1)}), bf16[16,2,384,256]{3,2,1,0:T(8,128)(2,1)}) %all-gather.7.cloned.1.call-update) | async-done | bytes 6291472 | tf_op jit(solution)/shard_map/all_gather | solution.py:42
  328.4 0.0 copy-done.1
  328.4 4.5 convolution_bitcast_fusion.1
  332.9 54.3 %psum.15 = f32[24,384]{1,0:T(8,128)S(1)} all-reduce(f32[24,384]{1,0:T(8,128)S(1)} %convolution_bitcast_fusion.1), channel_id=1, replica_groups=mesh['gx'=4,'gy'=16,'gz'=4] {'gx','gz'}, use_global_device_ids=true, to_apply=%region_2.0 | all-reduce | flops 9216 | bytes 73728 | tf_op jit(solution)/shard_map/psum | solution.py:46
  387.1 0.6 broadcast_multiply_fusion.1
  387.8 4.6 fusion
  392.3 99.6 %all-reduce.2.cloned.1.call-done = f32[384,1536]{1,0:T(8,128)} async-done(((f32[384,1536]{1,0:T(8,128)}), f32[384,1536]{1,0:T(8,128)}) %all-reduce.2.cloned.1.call-update) | async-done | bytes 2359312 | tf_op jit(solution)/shard_map/psum | solution.py:34
  491.9 3.3 broadcast_multiply_fusion
Async XLA Ops:
  7.2 96.4 %copy-start = (bf16[64,2,24,384]{3,2,1,0:T(8,128)(2,1)S(1)}, bf16[64,2,24,384]{3,2,1,0:T(8,128)(2,1)}, u32[]{:S(2)}) copy-start(bf16[64,2,24,384]{3,2,1,0:T(8,128)(2,1)} %param.3) | copy-start | bytes 7077892
  7.2 96.4 %all-gather.5.cloned.1.call-start = ((), (), s32[]{:S(2)}) async-start(), calls=%async_computation | async-start | bytes 11796480 | tf_op jit(solution)/shard_map/all_gather | solution.py:26
  7.9 200.6 %all-gather.9.cloned.1.call-start = ((), (), s32[]{:S(2)}) async-start(), calls=%async_computation.3 | async-start | bytes 11796480 | tf_op jit(solution)/shard_map/all_gather | solution.py:9
  111.4 0.9 copy-start.2
  111.4 217.0 %all-gather.7.cloned.1.call-start = ((), (), s32[]{:S(2)}) async-start(), calls=%async_computation.2 | async-start | bytes 6684672 | tf_op jit(solution)/shard_map/all_gather | solution.py:42
  124.9 367.0 %all-reduce.2.cloned.1.call-start = ((), (), s32[]{:S(2)}) async-start(), calls=%async_computation.1 | async-start | bytes 4718592 | tf_op jit(solution)/shard_map/psum | solution.py:34
  214.8 0.7 copy-start.3
  214.8 113.6 %copy-start.1 = (bf16[768,256]{1,0:T(8,128)(2,1)S(1)}, bf16[768,256]{1,0:T(8,128)(2,1)}, u32[]{:S(2)}) copy-start(bf16[768,256]{1,0:T(8,128)(2,1)} %convolution_convert_fusion) | copy-start | bytes 1179652
Sparse Core Ops, SparseCore 0:
  9.8 93.6 all-gather.4
  111.5 96.9 all-gather.8
  211.1 117.2 all-gather.6
  331.5 160.4 all-reduce.1
